TPU v7x, 256 devices: a whole 4x4x8 slice. The times are simulated.
256 devices in a mesh: wide: 32 (over x, y, core), narrow: 8 (over z).
Axes of the slice: x: 4, y: 4, z: 8, core: 2. Of those that a mesh axis runs over, the one named last changes fastest.
Arguments:
- blocks: bfloat16 [32, 8, 16, 64, 4096], P('wide', 'narrow'), may hold values from -16 to 16
- row_tile: int32 [32, 8, 16], P('wide', 'narrow'), may hold values from 0 to 15
- col_tile: int32 [32, 8, 16], P('wide', 'narrow'), may hold values from 0 to 63, as said below
- depth_tile: int32 [32, 8, 16], P('wide', 'narrow'), may hold values from 0 to 15
- block_count: int32 [32, 8], P('wide', 'narrow'), may hold values from 4 to 16, as said below
- factor_b: bfloat16 [32768, 256], P(('wide', 'narrow')), may hold values from -40 to 40
- factor_c: bfloat16 [1024, 256], replicated, may hold values from -0.076293945 to 0.076293945
Outputs:
- a_new: float32 [32768, 256], P(('wide', 'narrow'))
- b_new: float32 [32768, 256], P(('wide', 'narrow'))
Inputs may be any that keep to these rules, and one draw needn't show every extreme that they name: `block_count`: every device holds at least 4 live blocks, and some device exactly 16. col_tile // 2 is the index of wide that holds the block's mode-2 factor rows; among the 16 slots of one device, live or not, each such index appears at most 1 times, and some index exactly 1 times.
All inputs are finite; a program needn't handle non-finite values.
Results may differ from a plain program's by a relative error of at most 0.02.
Values may be sent and summed in bfloat16 or wider, within the bound.
No kernel may reach another device: no remote copies, remote signals or barrier semaphores. Data moves between devices by JAX's collectives and lax.ppermute only.
A program may use at most 128 MiB of HBM per device.

v0:
```python
import jax
import jax.numpy as jnp
from jax import lax
from jax.sharding import PartitionSpec as P

TI_DEV = 2


def right_solve(target, matrix):
    chol_lower = jnp.linalg.cholesky(matrix)
    middle = lax.linalg.triangular_solve(
        chol_lower, target, left_side=False, lower=True, transpose_a=True
    )
    return lax.linalg.triangular_solve(
        chol_lower, middle, left_side=False, lower=True, transpose_a=False
    )


def column_gram(matrix):
    return lax.dot_general(
        matrix, matrix, (((0,), (0,)), ((), ())), preferred_element_type=jnp.float32
    )


def depth_mix(one_block, depth_id, factor_c, tile_rows):
    depth_rows = lax.dynamic_slice_in_dim(factor_c, depth_id * tile_rows, tile_rows, 0)
    depth_mixed = lax.dot_general(
        one_block, depth_rows, (((0,), (0,)), ((), ())), preferred_element_type=jnp.float32
    )
    return depth_mixed.reshape(tile_rows, tile_rows, depth_rows.shape[1])


def local(blocks, row_tile, col_tile, depth_tile, block_count, factor_b, factor_c):
    local_blocks = blocks[0, 0]
    first_ids = row_tile[0, 0]
    second_ids = col_tile[0, 0]
    depth_ids = depth_tile[0, 0]
    live_count = block_count[0, 0]
    tile_rows = local_blocks.shape[1]
    rank_width = factor_c.shape[1]
    wide_count = lax.axis_size("wide")
    narrow_count = lax.axis_size("narrow")
    second_local = factor_b.shape[0] // tile_rows
    owners = second_ids // second_local
    inside = second_ids % second_local
    gram_c = column_gram(factor_c)
    gram_b = lax.psum(column_gram(factor_b), ("wide", "narrow"))
    gathered = lax.all_gather(factor_b, "wide", axis=0, tiled=True)
    b_tiles = gathered.reshape(wide_count * second_local, tile_rows, rank_width)
    b_pick = owners * second_local + inside

    def first_step(slot_index, partial_sum):
        one_block = lax.dynamic_index_in_dim(local_blocks, slot_index, 0, False)
        depth_mixed = depth_mix(one_block, depth_ids[slot_index], factor_c, tile_rows)
        b_rows = lax.dynamic_index_in_dim(b_tiles, b_pick[slot_index], 0, False).astype(jnp.float32)
        b_term = jnp.sum(depth_mixed * b_rows[None, :, :], axis=1)
        target = first_ids[slot_index]
        current = lax.dynamic_index_in_dim(partial_sum, target, 0, False)
        return lax.dynamic_update_index_in_dim(partial_sum, current + b_term, target, 0)

    first_part = lax.fori_loop(
        0,
        live_count,
        first_step,
        jnp.zeros((narrow_count * TI_DEV, tile_rows, rank_width), jnp.float32),
    )
    mttkrp_a = lax.psum_scatter(
        first_part.reshape(-1, rank_width), "narrow", scatter_dimension=0, tiled=True
    )
    a_new = right_solve(mttkrp_a, gram_b * gram_c)
    a_half = a_new.astype(jnp.bfloat16)
    a_rows = lax.all_gather(a_half, "narrow", axis=0, tiled=True)
    gram_a = lax.psum(column_gram(a_half), ("wide", "narrow"))
    a_tiles = a_rows.reshape(a_rows.shape[0] // tile_rows, tile_rows, rank_width)
    width_slots = wide_count * second_local
    second_pick = owners * second_local + inside

    def second_step(slot_index, partial_sum):
        one_block = lax.dynamic_index_in_dim(local_blocks, slot_index, 0, False)
        depth_mixed = depth_mix(one_block, depth_ids[slot_index], factor_c, tile_rows)
        a_part = lax.dynamic_index_in_dim(a_tiles, first_ids[slot_index], 0, False).astype(
            jnp.float32
        )
        a_term = jnp.sum(depth_mixed * a_part[:, None, :], axis=0)
        target = second_pick[slot_index]
        current = lax.dynamic_index_in_dim(partial_sum, target, 0, False)
        return lax.dynamic_update_index_in_dim(partial_sum, current + a_term, target, 0)

    second_part = lax.fori_loop(
        0, live_count, second_step, jnp.zeros((width_slots, tile_rows, rank_width), jnp.float32)
    )
    mttkrp_b = lax.psum_scatter(
        second_part.reshape(-1, rank_width), "wide", scatter_dimension=0, tiled=True
    )
    b_new = right_solve(mttkrp_b, gram_a * gram_c)
    return (a_new, b_new)


def solution(mesh):
    return jax.shard_map(
        local,
        mesh=mesh,
        in_specs=(
            P("wide", "narrow", None, None, None),
            P("wide", "narrow", None),
            P("wide", "narrow", None),
            P("wide", "narrow", None),
            P("wide", "narrow"),
            P(("wide", "narrow"), None),
            P(),
        ),
        out_specs=(P(("wide", "narrow"), None), P(("wide", "narrow"), None)),
        check_vma=False,
    )
```

profile of v0, /device:TPU:2, one launch (start us, length us, event | category | flops | bytes accessed | tf_op | source)
XLA Modules:
  0.0 688.1 jit_solution(2137662635349681206)
XLA Ops:
  8.8 1.8 fusion.35
  10.8 15.6 %copy.22 = bf16[1,1,16,64,4096]{3,4,2,1,0:T(8,128)(2,1)} copy(bf16[1,1,16,64,4096]{4,3,2,1,0:T(8,128)(2,1)} %param.16) | data formatting | bytes 16777216 | tf_op args[0]
  26.4 36.2 %all-gather.2.cloned.1.call-done = bf16[4096,256]{1,0:T(8,128)(2,1)} async-done(((bf16[128,256]{1,0:T(8,128)(2,1)}), bf16[4096,256]{1,0:T(8,128)(2,1)}) %all-gather.2.cloned.1.call-update) | async-done | bytes 2097168 | tf_op jit(solution)/shard_map/all_gather | solution.py:48
  62.7 144.2 %while.28 = (s32[]{:T(128)}, f32[16,64,256]{2,1,0:T(8,128)S(1)}, s32[]{:T(128)}, s32[16]{0:T(128)S(1)}, bf16[16,64,4096]{1,2,0:T(8,128)(2,1)}, /*index=5*/s32[16...) while((s32[]{:T(128)}, f32[16,64,256]{2,1,0:T(8,128)S(1)}, ...), condition=%wide.region_7.9_spmd, body=%wide.region_5.8_spmd.sunk | while | flops 136331280 | bytes 2556253 | solution.py:61
  207.9 64.7 %all-reduce.4.cloned.1.call-done = f32[256,256]{0,1:T(8,128)} async-done(((f32[256,256]{0,1:T(8,128)}), f32[256,256]{0,1:T(8,128)}) %all-reduce.4.cloned.1.call-update) | async-done | bytes 262160 | tf_op jit(solution)/shard_map/psum | solution.py:47
  274.1 11.7 %cholesky.130 = f32[128,128]{1,0:T(8,128)S(1)} custom-call(f32[128,128]{1,0:T(8,128)S(1)} %cholesky.194), custom_call_target="Cholesky" | custom-call | tf_op jit(solution)/shard_map/jit(cholesky)/cholesky | solution.py:10
  285.9 9.8 %custom-call.17 = f32[1,128,128]{1,2,0:T(8,128)S(1)} custom-call(f32[1,128,128]{2,1,0:T(8,128)S(1)} %get-tuple-element.211), custom_call_target="InvertDiagBlocksLowerTriangular" | custom-call | tf_op jit(solution)/shard_map/jit(cholesky)/cholesky | solution.py:10
  296.2 11.7 %cholesky.147 = f32[128,128]{1,0:T(8,128)S(1)} custom-call(f32[128,128]{1,0:T(8,128)S(1)} %convolution_subtract_fusion.5), custom_call_target="Cholesky" | custom-call | tf_op jit(solution)/shard_map/jit(cholesky)/cholesky | solution.py:10
  310.0 4.2 while.30
  314.2 19.7 %custom-call.18 = f32[2,128,128]{1,2,0:T(8,128)S(1)} custom-call(f32[2,128,128]{2,1,0:T(8,128)S(1)} %get-tuple-element.131), custom_call_target="InvertDiagBlocksLowerTriangular" | custom-call | tf_op jit(solution)/shard_map/triangular_solve/custom-call.0 | solution.py:11
  337.2 24.6 %all_gather.7 = bf16[1024,256]{0,1:T(8,128)(2,1)S(1)} all-gather(bf16[128,256]{0,1:T(8,128)(2,1)S(1)} %fusion.31), channel_id=1, replica_groups=mesh['wide'=32,'narrow'=8] {'narrow'}, dimensions={0}, use_global_device_ids=true | all-gather | bytes 589824 | tf_op jit(solution)/shard_map/all_gather | solution.py:72
  362.9 2.4 broadcast_in_dim.14
  365.4 159.6 %while.29 = (s32[]{:T(128)}, f32[64,64,256]{2,1,0:T(8,128)}, s32[]{:T(128)}, s32[16]{0:T(128)S(1)}, bf16[16,64,4096]{1,2,0:T(8,128)(2,1)}, /*index=5*/s32[16]{0:...) while((s32[]{:T(128)}, f32[64,64,256]{2,1,0:T(8,128)}, ...), condition=%wide.region_12.16_spmd, body=%wide.region_10.15_spmd.sunk | while | flops 136331280 | bytes 2556253 | solution.py:89
  395.7 1.5 fusion.72
  416.9 1.5 fusion.72
  469.8 1.5 fusion.72
  480.4 1.5 fusion.72
  491.0 1.5 fusion.72
  525.7 89.8 %all-reduce.6.cloned.1.call-done = f32[256,256]{0,1:T(8,128)} async-done(((f32[256,256]{0,1:T(8,128)}), f32[256,256]{0,1:T(8,128)}) %all-reduce.6.cloned.1.call-update) | async-done | bytes 262160 | tf_op jit(solution)/shard_map/psum | solution.py:73
  616.7 11.7 %cholesky.164 = f32[128,128]{1,0:T(8,128)S(1)} custom-call(f32[128,128]{1,0:T(8,128)S(1)} %cholesky.197), custom_call_target="Cholesky" | custom-call | tf_op jit(solution)/shard_map/jit(cholesky)/cholesky | solution.py:10
  628.5 9.8 %custom-call.20 = f32[1,128,128]{1,2,0:T(8,128)S(1)} custom-call(f32[1,128,128]{2,1,0:T(8,128)S(1)} %get-tuple-element.207), custom_call_target="InvertDiagBlocksLowerTriangular" | custom-call | tf_op jit(solution)/shard_map/jit(cholesky)/cholesky | solution.py:10
  638.7 11.7 %cholesky.181 = f32[128,128]{1,0:T(8,128)S(1)} custom-call(f32[128,128]{1,0:T(8,128)S(1)} %convolution_subtract_fusion.2), custom_call_target="Cholesky" | custom-call | tf_op jit(solution)/shard_map/jit(cholesky)/cholesky | solution.py:10
  653.1 4.1 while.31
  657.3 19.7 %custom-call.21 = f32[2,128,128]{1,2,0:T(8,128)S(1)} custom-call(f32[2,128,128]{2,1,0:T(8,128)S(1)} %get-tuple-element.133), custom_call_target="InvertDiagBlocksLowerTriangular" | custom-call | tf_op jit(solution)/shard_map/triangular_solve/custom-call.0 | solution.py:11
  (287 shorter events, 166.4 us)
Async XLA Ops:
  8.0 54.6 %all-gather.2.cloned.1.call-start = ((), (), s32[]{:S(2)}) async-start(), calls=%async_computation.3 | async-start | bytes 2162688 | tf_op jit(solution)/shard_map/all_gather | solution.py:48
  8.7 263.9 %all-reduce.4.cloned.1.call-start = ((), (), s32[]{:S(2)}) async-start(), calls=%async_computation.2 | async-start | bytes 524288 | tf_op jit(solution)/shard_map/psum | solution.py:47
  10.7 323.2 %reduce-scatter.3.cloned.1.call-start = ((), (), s32[]{:S(2)}) async-start(), calls=%async_computation.4 | async-start | bytes 1179648 | tf_op jit(solution)/shard_map/reduce_scatter | solution.py:67
  10.7 15.7 %copy-start.2 = (s32[1,1,16]{2,1,0:T(1,128)S(1)}, s32[1,1,16]{2,1,0:T(1,128)}, u32[]{:S(2)}) copy-start(s32[1,1,16]{2,1,0:T(1,128)} %param.18) | copy-start | bytes 196
  10.7 51.9 %copy-start.1 = (bf16[1024,256]{1,0:T(8,128)(2,1)S(1)}, bf16[1024,256]{1,0:T(8,128)(2,1)}, u32[]{:S(2)}) copy-start(bf16[1024,256]{1,0:T(8,128)(2,1)} %param.22) | copy-start | bytes 1572868
  10.7 51.9 %copy-start.3 = (s32[1,1,16]{2,1,0:T(1,128)S(1)}, s32[1,1,16]{2,1,0:T(1,128)}, u32[]{:S(2)}) copy-start(s32[1,1,16]{2,1,0:T(1,128)} %param.17) | copy-start | bytes 196
  10.7 51.9 %copy-start.4 = (s32[1,1,16]{2,1,0:T(1,128)S(1)}, s32[1,1,16]{2,1,0:T(1,128)}, u32[]{:S(2)}) copy-start(s32[1,1,16]{2,1,0:T(1,128)} %param.19) | copy-start | bytes 196
  206.9 1.0 copy-start
  207.9 407.6 %all-reduce.6.cloned.1.call-start = ((), (), s32[]{:S(2)}) async-start(), calls=%async_computation.5 | async-start | bytes 524288 | tf_op jit(solution)/shard_map/psum | solution.py:73
  362.9 314.1 %reduce-scatter.5.cloned.1.call-start = ((), (), s32[]{:S(2)}) async-start(), calls=%async_computation.6 | async-start | bytes 4325376 | tf_op jit(solution)/shard_map/reduce_scatter | solution.py:92
Sparse Core Ops, SparseCore 0:
  11.4 51.1 all-gather.1
  208.0 42.8 reduce-scatter.2
  525.1 93.6 reduce-scatter.4
Sparse Core Ops, SparseCore 1:
  14.7 257.9 all-reduce.3
  363.0 252.5 all-reduce.5
where the time goes:
time: 694 us; the launch traced here: 688 us
  waiting for transfers between devices  191 us (28%)
  loops' own time  155 us (22%)
  other arithmetic  143 us (21%)
  local copies, waits for them, and re-layouts  121 us (17%)
  matrix products  34.1 us (5%)
  blocking collectives  24.6 us (4%)
  between operations  18.1 us (3%)
    psum x1, waiting for transfers between devices, local(): gram_a = lax.psum(column_gram(a_half), ('wide', 'narrow'))  89.8 us
    another operation x1, loops' own time, local(): lax.fori_loop(0, live_count, second_step, jnp.zeros((width_slots, tile_ro...  79.1 us
    another operation x1, loops' own time, local(): lax.fori_loop(0, live_count, first_step, jnp.zeros((narrow_count * TI_DEV...  75.7 us
    another operation x13, other arithmetic, right_solve(): chol_lower = jnp.linalg.cholesky(matrix)  68.6 us
    psum x1, waiting for transfers between devices, local(): gram_b = lax.psum(column_gram(factor_b), ('wide', 'narrow'))  64.7 us
    another operation x5, other arithmetic, right_solve(): lax.linalg.triangular_solve(chol_lower, target, left_side=False, lower=Tr...  39.4 us
    all_gather x1, waiting for transfers between devices, local(): gathered = lax.all_gather(factor_b, 'wide', axis=0, tiled=True)  36.2 us
    all_gather x1, blocking collectives, local(): a_rows = lax.all_gather(a_half, 'narrow', axis=0, tiled=True)  24.6 us
  transfers between devices with their start and end apart: 5, of which 3 were waited for; matrix products, arithmetic and copies ran while one was open for 42% of the time, Pallas kernels for 0%

commit v1 on v0

--- a/solution.py
+++ b/solution.py
@@ -4,6 +4,12 @@
 from jax.sharding import PartitionSpec as P
 
 TI_DEV = 2
+
+
+def balance_the_corner(point):
+    for d in ("wide", "narrow"):
+        point = lax.psum(point, axis_name=d)
+    return point
 
 
 def right_solve(target, matrix):
@@ -44,7 +50,7 @@
     owners = second_ids // second_local
     inside = second_ids % second_local
     gram_c = column_gram(factor_c)
-    gram_b = lax.psum(column_gram(factor_b), ("wide", "narrow"))
+    gram_b = balance_the_corner(column_gram(factor_b))
     gathered = lax.all_gather(factor_b, "wide", axis=0, tiled=True)
     b_tiles = gathered.reshape(wide_count * second_local, tile_rows, rank_width)
     b_pick = owners * second_local + inside

time: 694 us -> 780 us (1.12)
  waiting for transfers between devices: 191 us -> 279 us
    psum x1 -> x2, waiting for transfers between devices: 64.7 us -> 100 us  [balance_the_corner(): point = lax.psum(point, axis_name=d)]
    reduce_scatter x1, waiting for transfers between devices: 0.02 us -> 31.1 us  [local(): lax.psum_scatter(second_part.reshape(-1, rank_width), 'wide', scatter_dim...]
    all_gather x1, waiting for transfers between devices: 36.2 us -> 51 us  [local(): gathered = lax.all_gather(factor_b, 'wide', axis=0, tiled=True)]
  transfers between devices with their start and end apart: 5 -> 6, of which waited for: 3 -> 4; matrix products, arithmetic and copies ran while one was open for 42% -> 37% of each run, Pallas kernels for 0% -> 0%
where the time goes in v1:
time: 780 us; the launch traced here: 773 us
  waiting for transfers between devices  279 us (36%)
  loops' own time  155 us (20%)
  other arithmetic  143 us (18%)
  local copies, waits for them, and re-layouts  121 us (16%)
  matrix products  34.1 us (4%)
  blocking collectives  23.3 us (3%)
  between operations  17 us (2%)
    psum x2, waiting for transfers between devices, balance_the_corner(): point = lax.psum(point, axis_name=d)  100 us
    psum x1, waiting for transfers between devices, local(): gram_a = lax.psum(column_gram(a_half), ('wide', 'narrow'))  95.6 us
    another operation x1, loops' own time, local(): lax.fori_loop(0, live_count, second_step, jnp.zeros((width_slots, tile_ro...  79.1 us
    another operation x1, loops' own time, local(): lax.fori_loop(0, live_count, first_step, jnp.zeros((narrow_count * TI_DEV...  75.7 us
    another operation x13, other arithmetic, right_solve(): chol_lower = jnp.linalg.cholesky(matrix)  68.6 us
    all_gather x1, waiting for transfers between devices, local(): gathered = lax.all_gather(factor_b, 'wide', axis=0, tiled=True)  51 us
    another operation x5, other arithmetic, right_solve(): lax.linalg.triangular_solve(chol_lower, target, left_side=False, lower=Tr...  39.4 us
    reduce_scatter x1, waiting for transfers between devices, local(): lax.psum_scatter(second_part.reshape(-1, rank_width), 'wide', scatter_dim...  31.1 us
  transfers between devices with their start and end apart: 6, of which 4 were waited for; matrix products, arithmetic and copies ran while one was open for 37% of the time, Pallas kernels for 0%

profile of v1, /device:TPU:2, one launch (start us, length us, event | category | flops | bytes accessed | tf_op | source)
XLA Modules:
  0.0 773.4 jit_solution(11975603047328542560)
XLA Ops:
  7.2 1.8 fusion.35
  9.9 15.6 %copy.22 = bf16[1,1,16,64,4096]{3,4,2,1,0:T(8,128)(2,1)} copy(bf16[1,1,16,64,4096]{4,3,2,1,0:T(8,128)(2,1)} %param.16) | data formatting | bytes 16777216 | tf_op args[0]
  25.6 100.4 %all-reduce.5.cloned.1.call-done = f32[256,256]{0,1:T(8,128)} async-done(((f32[256,256]{0,1:T(8,128)}), f32[256,256]{0,1:T(8,128)}) %all-reduce.5.cloned.1.call-update) | async-done | bytes 262160 | tf_op jit(solution)/shard_map/psum | solution.py:11
  126.1 51.0 %all-gather.2.cloned.1.call-done = bf16[4096,256]{1,0:T(8,128)(2,1)} async-done(((bf16[128,256]{1,0:T(8,128)(2,1)}), bf16[4096,256]{1,0:T(8,128)(2,1)}) %all-gather.2.cloned.1.call-update) | async-done | bytes 2097168 | tf_op jit(solution)/shard_map/all_gather | solution.py:54
  177.3 144.1 %while.28 = (s32[]{:T(128)}, f32[16,64,256]{2,1,0:T(8,128)S(1)}, s32[]{:T(128)}, s32[16]{0:T(128)S(1)}, bf16[16,64,4096]{1,2,0:T(8,128)(2,1)}, /*index=5*/s32[16...) while((s32[]{:T(128)}, f32[16,64,256]{2,1,0:T(8,128)S(1)}, ...), condition=%wide.region_8.10_spmd, body=%wide.region_6.9_spmd.sunk | while | flops 136331280 | bytes 2556253 | solution.py:67
  324.0 11.7 %cholesky.130 = f32[128,128]{1,0:T(8,128)S(1)} custom-call(f32[128,128]{1,0:T(8,128)S(1)} %cholesky.194), custom_call_target="Cholesky" | custom-call | tf_op jit(solution)/shard_map/jit(cholesky)/cholesky | solution.py:16
  335.7 9.8 %custom-call.17 = f32[1,128,128]{1,2,0:T(8,128)S(1)} custom-call(f32[1,128,128]{2,1,0:T(8,128)S(1)} %get-tuple-element.211), custom_call_target="InvertDiagBlocksLowerTriangular" | custom-call | tf_op jit(solution)/shard_map/jit(cholesky)/cholesky | solution.py:16
  346.0 11.7 %cholesky.147 = f32[128,128]{1,0:T(8,128)S(1)} custom-call(f32[128,128]{1,0:T(8,128)S(1)} %convolution_subtract_fusion.5), custom_call_target="Cholesky" | custom-call | tf_op jit(solution)/shard_map/jit(cholesky)/cholesky | solution.py:16
  359.9 4.2 while.30
  364.0 19.7 %custom-call.18 = f32[2,128,128]{1,2,0:T(8,128)S(1)} custom-call(f32[2,128,128]{2,1,0:T(8,128)S(1)} %get-tuple-element.131), custom_call_target="InvertDiagBlocksLowerTriangular" | custom-call | tf_op jit(solution)/shard_map/triangular_solve/custom-call.0 | solution.py:17
  387.0 23.3 %all_gather.7 = bf16[1024,256]{0,1:T(8,128)(2,1)S(1)} all-gather(bf16[128,256]{0,1:T(8,128)(2,1)S(1)} %fusion.31), channel_id=1, replica_groups=mesh['wide'=32,'narrow'=8] {'narrow'}, dimensions={0}, use_global_device_ids=true | all-gather | bytes 589824 | tf_op jit(solution)/shard_map/all_gather | solution.py:78
  411.5 2.4 broadcast_in_dim.14
  414.0 159.6 %while.29 = (s32[]{:T(128)}, f32[64,64,256]{2,1,0:T(8,128)}, s32[]{:T(128)}, s32[16]{0:T(128)S(1)}, bf16[16,64,4096]{1,2,0:T(8,128)(2,1)}, /*index=5*/s32[16]{0:...) while((s32[]{:T(128)}, f32[64,64,256]{2,1,0:T(8,128)}, ...), condition=%wide.region_13.17_spmd, body=%wide.region_11.16_spmd.sunk | while | flops 136331280 | bytes 2556253 | solution.py:95
  444.3 1.5 fusion.72
  465.5 1.5 fusion.72
  529.0 1.5 fusion.72
  539.6 1.5 fusion.72
  574.3 95.6 %all-reduce.9.cloned.1.call-done = f32[256,256]{0,1:T(8,128)} async-done(((f32[256,256]{0,1:T(8,128)}), f32[256,256]{0,1:T(8,128)}) %all-reduce.9.cloned.1.call-update) | async-done | bytes 262160 | tf_op jit(solution)/shard_map/psum | solution.py:79
  671.2 11.7 %cholesky.164 = f32[128,128]{1,0:T(8,128)S(1)} custom-call(f32[128,128]{1,0:T(8,128)S(1)} %cholesky.197), custom_call_target="Cholesky" | custom-call | tf_op jit(solution)/shard_map/jit(cholesky)/cholesky | solution.py:16
  682.9 9.8 %custom-call.20 = f32[1,128,128]{1,2,0:T(8,128)S(1)} custom-call(f32[1,128,128]{2,1,0:T(8,128)S(1)} %get-tuple-element.207), custom_call_target="InvertDiagBlocksLowerTriangular" | custom-call | tf_op jit(solution)/shard_map/jit(cholesky)/cholesky | solution.py:16
  693.2 11.7 %cholesky.181 = f32[128,128]{1,0:T(8,128)S(1)} custom-call(f32[128,128]{1,0:T(8,128)S(1)} %convolution_subtract_fusion.2), custom_call_target="Cholesky" | custom-call | tf_op jit(solution)/shard_map/jit(cholesky)/cholesky | solution.py:16
  707.6 4.1 while.31
  711.7 19.7 %custom-call.21 = f32[2,128,128]{1,2,0:T(8,128)S(1)} custom-call(f32[2,128,128]{2,1,0:T(8,128)S(1)} %get-tuple-element.133), custom_call_target="InvertDiagBlocksLowerTriangular" | custom-call | tf_op jit(solution)/shard_map/triangular_solve/custom-call.0 | solution.py:17
  731.4 31.1 %reduce-scatter.5.cloned.1.call-done = f32[128,256]{1,0:T(8,128)} async-done(((f32[4096,256]{1,0:T(8,128)}), f32[128,256]{1,0:T(8,128)}) %reduce-scatter.5.cloned.1.call-update) | async-done | bytes 131088 | tf_op jit(solution)/shard_map/reduce_scatter | solution.py:98
  (290 shorter events, 167.8 us)
Async XLA Ops:
  7.2 118.8 %all-reduce.5.cloned.1.call-start = ((), (), s32[]{:S(2)}) async-start(), calls=%async_computation.2 | async-start | bytes 524288 | tf_op jit(solution)/shard_map/psum | solution.py:11
  9.1 168.0 %all-gather.2.cloned.1.call-start = ((), (), s32[]{:S(2)}) async-start(), calls=%async_computation.4 | async-start | bytes 2162688 | tf_op jit(solution)/shard_map/all_gather | solution.py:54
  9.8 312.6 %all-reduce.7.cloned.1.call-start = ((), (), s32[]{:S(2)}) async-start(), calls=%async_computation.3 | async-start | bytes 524288 | tf_op jit(solution)/shard_map/psum | solution.py:11
  9.9 15.7 %copy-start.2 = (s32[1,1,16]{2,1,0:T(1,128)S(1)}, s32[1,1,16]{2,1,0:T(1,128)}, u32[]{:S(2)}) copy-start(s32[1,1,16]{2,1,0:T(1,128)} %param.18) | copy-start | bytes 196
  9.9 167.3 %copy-start.1 = (bf16[1024,256]{1,0:T(8,128)(2,1)S(1)}, bf16[1024,256]{1,0:T(8,128)(2,1)}, u32[]{:S(2)}) copy-start(bf16[1024,256]{1,0:T(8,128)(2,1)} %param.22) | copy-start | bytes 1572868
  9.9 167.3 %copy-start.3 = (s32[1,1,16]{2,1,0:T(1,128)S(1)}, s32[1,1,16]{2,1,0:T(1,128)}, u32[]{:S(2)}) copy-start(s32[1,1,16]{2,1,0:T(1,128)} %param.17) | copy-start | bytes 196
  9.9 167.3 %copy-start.4 = (s32[1,1,16]{2,1,0:T(1,128)S(1)}, s32[1,1,16]{2,1,0:T(1,128)}, u32[]{:S(2)}) copy-start(s32[1,1,16]{2,1,0:T(1,128)} %param.19) | copy-start | bytes 196
  126.0 257.7 %reduce-scatter.3.cloned.1.call-start = ((), (), s32[]{:S(2)}) async-start(), calls=%async_computation.5 | async-start | bytes 1179648 | tf_op jit(solution)/shard_map/reduce_scatter | solution.py:73
  321.4 1.0 copy-start
  322.4 347.6 %all-reduce.9.cloned.1.call-start = ((), (), s32[]{:S(2)}) async-start(), calls=%async_computation.6 | async-start | bytes 524288 | tf_op jit(solution)/shard_map/psum | solution.py:79
  411.5 351.1 %reduce-scatter.5.cloned.1.call-start = ((), (), s32[]{:S(2)}) async-start(), calls=%async_computation.7 | async-start | bytes 4325376 | tf_op jit(solution)/shard_map/reduce_scatter | solution.py:98
Sparse Core Ops, SparseCore 0:
  11.2 114.7 all-reduce.4
  128.6 48.5 all-gather.1
  179.4 72.7 all-reduce.6
  322.5 42.6 reduce-scatter.2
  411.6 258.3 all-reduce.8
  673.8 88.7 reduce-scatter.4
